TPU v7x, 512 devices: a whole 4x4x16 slice. The times are simulated.
512 devices in a mesh: row: 16 (over y, x), col: 32 (over z, core).
Axes of the slice: x: 4, y: 4, z: 16, core: 2. Of those that a mesh axis runs over, the one named last changes fastest.
Arguments:
- tokens: bfloat16 [4096, 8192], P('row', 'col'), may hold values from -6 to 6
- w_in: bfloat16 [8192, 3, 8192], P('row', None, 'col'), may hold values from -0.0625 to 0.0625
- filt_in: float32 [7, 3, 8192], P(None, None, 'col'), may hold values from -2.4 to 2.4
- filt_mix: float32 [7, 8192], P(None, 'col'), may hold values from -2.4 to 2.4
Outputs:
- gated: bfloat16 [4096, 8192], P('row', 'col')
All inputs are finite; a program needn't handle non-finite values.
Results may differ from a plain program's by a relative error of at most 0.0064.
Values may be sent and summed in bfloat16 or wider, within the bound.
A program may use at most 64 MiB of HBM per device.

v0:
```python
import jax
import jax.numpy as jnp
from jax import lax
from jax.sharding import PartitionSpec as P


def passed_along(block, axis, distance):
    devices = range(lax.axis_size(axis))
    route = [(i - distance, i) for i in devices if i - distance in devices]
    return lax.ppermute(block, axis, route)


def taps(ext, filt, count):
    total = filt[0] * ext[6 : 6 + count]
    for shift_s in range(1, 7):
        total = total + filt[shift_s] * ext[6 - shift_s : 6 - shift_s + count]
    return total


def per_device(tokens, w_in, filt_in, filt_mix):
    rows = tokens.shape[0]
    cols = w_in.shape[2]
    strip = lax.all_gather(tokens, "col", axis=1, tiled=True)
    piece = lax.all_gather(w_in, "row", axis=0, tiled=True)
    flat_piece = piece.reshape(piece.shape[0], 3 * cols)
    summed = jnp.dot(strip, flat_piece, preferred_element_type=jnp.float32)
    proj = summed.astype(jnp.bfloat16).reshape(rows, 3, cols)
    starts_seq = lax.axis_index("row") == 0
    keep_f = jnp.where(starts_seq, 0.0, 1.0).astype(jnp.float32)
    rim = passed_along(proj[rows - 6 :], "row", 1)
    ext = jnp.concatenate([rim.astype(jnp.float32) * keep_f, proj.astype(jnp.float32)], axis=0)
    conv = taps(ext, filt_in, rows)
    prod = conv[:, 1] * conv[:, 2]
    prod_rim = passed_along(prod[rows - 6 :], "row", 1)
    ext_prod = jnp.concatenate([prod_rim * keep_f, prod], axis=0)
    mix = taps(ext_prod, filt_mix, rows)
    query = conv[:, 0]
    return (query * mix).astype(jnp.bfloat16)


def solution(mesh):
    return jax.shard_map(
        per_device,
        mesh=mesh,
        in_specs=(P("row", "col"), P("row", None, "col"), P(None, None, "col"), P(None, "col")),
        out_specs=P("row", "col"),
        check_vma=False,
    )
```

profile of v0, /device:TPU:8, one launch (start us, length us, event | category | flops | bytes accessed | tf_op | source)
XLA Modules:
  0.0 247.7 jit_solution(13775816980189097958)
XLA Ops:
  6.5 0.0 all-gather.3.cloned.1.call-start
  6.5 0.7 all-gather.3.cloned.1.call-update
  7.3 0.0 all-gather.5.cloned.1.call-start
  7.3 2.3 copy.8
  9.6 0.0 all-gather.5.cloned.1.call-update
  9.6 1.0 fusion.36
  10.7 83.2 %all-gather.3.cloned.1.call-done = bf16[256,8192]{1,0:T(8,128)(2,1)} async-done(((bf16[256,256]{1,0:T(8,128)(2,1)}), bf16[256,8192]{1,0:T(8,128)(2,1)}) %all-gather.3.cloned.1.call-update) | async-done | bytes 4194320 | tf_op jit(solution)/shard_map/all_gather | solution.py:23
  93.9 114.1 %all-gather.5.cloned.1.call-done = bf16[8192,3,256]{0,2,1:T(8,128)(2,1)} async-done(((bf16[512,3,256]{0,2,1:T(8,128)(2,1)}), bf16[8192,3,256]{0,2,1:T(8,128)(2,1)}) %all-gather.5.cloned.1.call-update) | async-done | bytes 12582928 | tf_op jit(solution)/shard_map/all_gather | solution.py:24
  208.0 0.0 copy-start
  208.0 9.3 %convolution_convert_fusion = bf16[256,768]{1,0:T(8,128)(2,1)S(1)} fusion(bf16[256,8192]{1,0:T(8,128)(2,1)} %all-gather.3.cloned.1.call-done, bf16[8192,768]{0,1:T(8,128)(2,1)} %bitcast.45), kind=kOutput, calls=%fused_computation.10 | convolution fusion | flops 3221422080 | bytes 17170432 | tf_op jit(solution)/shard_map/dot_general | solution.py:26
  217.3 0.2 copy.12
  217.5 2.2 collective-permute-start
  219.7 0.0 copy-done
  219.8 0.2 copy.9
  219.9 7.3 %collective-permute-done = bf16[6,3,256]{0,2,1:T(8,128)(2,1)S(1)} collective-permute-done((bf16[6,3,256]{0,2,1:T(8,128)(2,1)S(1)}, bf16[6,3,256]{0,2,1:T(8,128)(2,1)S(1)}, u32[]{:S(2)}, u32[]{:S(2)}) %collective-permute-start) | collective-permute-done | bytes 9248 | tf_op jit(solution)/shard_map/ppermute | solution.py:10
  227.3 2.7 %fusion.3 = f32[256,3,256]{0,2,1:T(8,128)S(1)} fusion(f32[256,3,256]{0,2,1:T(8,128)S(1)} %bitcast.35, f32[6,3,256]{0,2,1:T(8,128)S(1)} %convert_multiply_fusion, f32[3,256]{1,0:T(4,128)S(1)} %get-tuple-element.19, f32[3,256]{1,0:T(4,128)S(1)} %get-tuple-element.20, f32[3,256]{1,0:T(4,128)S(1)} %get-tuple-element.21, f32[3,256]{1,0:T(4,128)S(1)} %get-tuple-element.22, ...), kind=kLoop, calls=%fused_computation.19 | loop fusion | flops 3735552 | bytes 1612800 | tf_op jit(solution)/shard_map/add | solution.py:16
  230.1 0.1 slice_bitcast_fusion.1
  230.2 1.9 collective-permute-start.1
  232.1 7.0 %collective-permute-done.1 = f32[6,256]{0,1:T(8,128)S(1)} collective-permute-done((f32[6,256]{0,1:T(8,128)S(1)}, f32[6,256]{0,1:T(8,128)S(1)}, u32[]{:S(2)}, u32[]{:S(2)}) %collective-permute-start.1) | collective-permute-done | bytes 6176 | tf_op jit(solution)/shard_map/ppermute | solution.py:10
  239.2 0.9 fusion.22
  240.1 0.8 copy.11
  (10 shorter events, 0.1 us)
Async XLA Ops:
  6.5 87.4 %all-gather.3.cloned.1.call-start = ((), (), s32[]{:S(2)}) async-start(), calls=%async_computation | async-start | bytes 4325376 | tf_op jit(solution)/shard_map/all_gather | solution.py:23
  7.3 200.7 %all-gather.5.cloned.1.call-start = ((), (), s32[]{:S(2)}) async-start(), calls=%async_computation.1 | async-start | bytes 13369344 | tf_op jit(solution)/shard_map/all_gather | solution.py:24
  208.0 11.7 %copy-start = (f32[7,256]{1,0:T(8,128)S(1)}, f32[7,256]{1,0:T(8,128)}, u32[]{:S(2)}) copy-start(f32[7,256]{1,0:T(8,128)} %param.7) | copy-start | bytes 21508
  217.5 9.8 %collective-permute-start = (bf16[6,3,256]{0,2,1:T(8,128)(2,1)S(1)}, bf16[6,3,256]{0,2,1:T(8,128)(2,1)S(1)}, u32[]{:S(2)}, u32[]{:S(2)}) collective-permute-start(bf16[6,3,256]{0,2,1:T(8,128)(2,1)S(1)} %bitcast.36), channel_id=1, source_target_pairs={{0,32},{32,64},{64,96},{96,128},{128,160},{160,192},{192,224},{224... | collective-permute-start | bytes 27656 | tf_op jit(solution)/shard_map/ppermute | solution.py:10
  230.2 9.0 %collective-permute-start.1 = (f32[6,256]{0,1:T(8,128)S(1)}, f32[6,256]{0,1:T(8,128)S(1)}, u32[]{:S(2)}, u32[]{:S(2)}) collective-permute-start(f32[6,256]{0,1:T(8,128)S(1)} %slice_bitcast_fusion.1), channel_id=1, source_target_pairs={{0,32},{32,64},{64,96},{96,128},{128,160},{160,192},{192,224},{224... | collective-permute-start | bytes 18440 | tf_op jit(solution)/shard_map/ppermute | solution.py:10
Sparse Core Ops, SparseCore 0:
  9.4 84.4 all-gather.2
  96.9 111.0 all-gather.4
where the time goes:
time: 248 us
  waiting for transfers between devices  212 us (85%)
  between operations  13.5 us (5%)
  matrix products  9.31 us (4%)
  local copies, waits for them, and re-layouts  4.56 us (2%)
  starting transfers between devices  4.17 us (2%)
  other arithmetic  3.72 us (2%)
    all_gather x1, waiting for transfers between devices, per_device(): piece = lax.all_gather(w_in, 'row', axis=0, tiled=True)  114 us
    all_gather x1, waiting for transfers between devices, per_device(): strip = lax.all_gather(tokens, 'col', axis=1, tiled=True)  83.2 us
    ppermute x2, waiting for transfers between devices, passed_along(): return lax.ppermute(block, axis, route)  14.3 us
    dot_general x1, matrix products, per_device(): summed = jnp.dot(strip, flat_piece, preferred_element_type=jnp.float32)  9.31 us
  transfers between devices with their start and end apart: 4, of which 4 were waited for; matrix products, arithmetic and copies ran while one was open for 1% of the time, Pallas kernels for 0%

commit v1 on v0

--- a/solution.py
+++ b/solution.py
@@ -20,7 +20,10 @@
 def per_device(tokens, w_in, filt_in, filt_mix):
     rows = tokens.shape[0]
     cols = w_in.shape[2]
-    strip = lax.all_gather(tokens, "col", axis=1, tiled=True)
+    count_2 = lax.axis_size("col")
+    blocks = jnp.stack([tokens for _ in range(count_2)])
+    blocks = lax.all_to_all(blocks, "col", split_axis=0, concat_axis=0)
+    strip = jnp.concatenate(blocks, axis=1)
     piece = lax.all_gather(w_in, "row", axis=0, tiled=True)
     flat_piece = piece.reshape(piece.shape[0], 3 * cols)
     summed = jnp.dot(strip, flat_piece, preferred_element_type=jnp.float32)

time: 248 us -> 258 us (1.040)
  the two profiles are of different devices: /device:TPU:8 before, /device:TPU:40 now
where the time goes in v1:
time: 258 us
  waiting for transfers between devices  203 us (79%)
  starting transfers between devices  20.9 us (8%)
  between operations  13.6 us (5%)
  matrix products  9.34 us (4%)
  local copies, waits for them, and re-layouts  6.97 us (3%)
  other arithmetic  3.72 us (1%)
    all_to_all x1, waiting for transfers between devices, per_device(): blocks = lax.all_to_all(blocks, 'col', split_axis=0, concat_axis=0)  190 us
    all_to_all x1, starting transfers between devices, per_device(): blocks = lax.all_to_all(blocks, 'col', split_axis=0, concat_axis=0)  15.5 us
    ppermute x2, waiting for transfers between devices, passed_along(): return lax.ppermute(block, axis, route)  13 us
    dot_general x1, matrix products, per_device(): summed = jnp.dot(strip, flat_piece, preferred_element_type=jnp.float32)  9.34 us
    ppermute x2, starting transfers between devices, passed_along(): return lax.ppermute(block, axis, route)  5.32 us
  transfers between devices with their start and end apart: 4, of which 3 were waited for; matrix products, arithmetic and copies ran while one was open for 1% of the time, Pallas kernels for 0%

profile of v1, /device:TPU:40, one launch (start us, length us, event | category | flops | bytes accessed | tf_op | source)
XLA Modules:
  0.0 257.6 jit_solution(8381977825179619971)
XLA Ops:
  6.5 0.0 all-gather.2.cloned.1.call-start
  6.5 2.3 copy.9
  8.8 0.0 all-gather.2.cloned.1.call-update
  8.9 1.0 copy.8
  9.9 2.4 stack.2
  12.3 0.0 copy-start
  12.3 15.5 %all-to-all-start = ((bf16[32,256,256]{1,2,0:T(8,128)(2,1)}), bf16[32,256,256]{1,2,0:T(8,128)(2,1)}, u32[]{:S(2)}, u32[]{:S(2)}) async-start(bf16[32,256,256]{1,2,0:T(8,128)(2,1)} %stack.2), calls=%async_computation | async-start | bytes 8388608 | tf_op jit(solution)/shard_map/all_to_all | solution.py:25
  27.8 0.0 copy-done
  27.9 190.1 %all-to-all-done = bf16[32,256,256]{1,2,0:T(8,128)(2,1)} async-done(((bf16[32,256,256]{1,2,0:T(8,128)(2,1)}), bf16[32,256,256]{1,2,0:T(8,128)(2,1)}, u32[]{:S(2)}, u32[]{:S(2)}) %all-to-all-start) | async-done | bytes 4194336 | tf_op jit(solution)/shard_map/all_to_all | solution.py:25
  218.0 0.0 all-gather.2.cloned.1.call-done
  218.0 0.0 copy-start.1
  218.0 9.3 %convolution_convert_fusion = bf16[256,768]{1,0:T(8,128)(2,1)S(1)} fusion(bf16[256,8192]{0,1:T(8,128)(2,1)} %bitcast.1, bf16[8192,768]{0,1:T(8,128)(2,1)} %bitcast.48), kind=kOutput, calls=%fused_computation.10 | convolution fusion | flops 3221422080 | bytes 17170432 | tf_op jit(solution)/shard_map/dot_general | solution.py:29
  227.4 0.2 copy.13
  227.5 3.4 %collective-permute-start = (bf16[6,3,256]{0,2,1:T(8,128)(2,1)S(1)}, bf16[6,3,256]{0,2,1:T(8,128)(2,1)S(1)}, u32[]{:S(2)}, u32[]{:S(2)}) collective-permute-start(bf16[6,3,256]{0,2,1:T(8,128)(2,1)S(1)} %bitcast.39), channel_id=1, source_target_pairs={{0,32},{32,64},{64,96},{96,128},{128,160},{160,192},{192,224},{224... | collective-permute-start | bytes 27656 | tf_op jit(solution)/shard_map/ppermute | solution.py:10
  230.9 0.0 copy-done.1
  231.0 0.2 copy.10
  231.2 6.0 %collective-permute-done = bf16[6,3,256]{0,2,1:T(8,128)(2,1)S(1)} collective-permute-done((bf16[6,3,256]{0,2,1:T(8,128)(2,1)S(1)}, bf16[6,3,256]{0,2,1:T(8,128)(2,1)S(1)}, u32[]{:S(2)}, u32[]{:S(2)}) %collective-permute-start) | collective-permute-done | bytes 9248 | tf_op jit(solution)/shard_map/ppermute | solution.py:10
  237.2 2.7 %fusion.3 = f32[256,3,256]{0,2,1:T(8,128)S(1)} fusion(f32[256,3,256]{0,2,1:T(8,128)S(1)} %bitcast.38, f32[6,3,256]{0,2,1:T(8,128)S(1)} %convert_multiply_fusion, f32[3,256]{1,0:T(4,128)S(1)} %get-tuple-element.19, f32[3,256]{1,0:T(4,128)S(1)} %get-tuple-element.20, f32[3,256]{1,0:T(4,128)S(1)} %get-tuple-element.21, f32[3,256]{1,0:T(4,128)S(1)} %get-tuple-element.22, ...), kind=kLoop, calls=%fused_computation.19 | loop fusion | flops 3735552 | bytes 1612800 | tf_op jit(solution)/shard_map/add | solution.py:16
  240.0 0.1 slice_bitcast_fusion.1
  240.1 1.9 collective-permute-start.1
  242.1 7.0 %collective-permute-done.1 = f32[6,256]{0,1:T(8,128)S(1)} collective-permute-done((f32[6,256]{0,1:T(8,128)S(1)}, f32[6,256]{0,1:T(8,128)S(1)}, u32[]{:S(2)}, u32[]{:S(2)}) %collective-permute-start.1) | collective-permute-done | bytes 6176 | tf_op jit(solution)/shard_map/ppermute | solution.py:10
  249.1 0.9 fusion.22
  250.0 0.8 copy.12
  (11 shorter events, 0.2 us)
Async XLA Ops:
  6.5 211.5 %all-gather.2.cloned.1.call-start = ((), (), s32[]{:S(2)}) async-start(), calls=%async_computation.1 | async-start | bytes 13369344 | tf_op jit(solution)/shard_map/all_gather | solution.py:27
  12.3 15.6 %copy-start = (f32[7,3,256]{2,0,1:T(8,128)S(1)}, f32[7,3,256]{2,0,1:T(8,128)}, u32[]{:S(2)}) copy-start(f32[7,3,256]{2,0,1:T(8,128)} %param.6) | copy-start | bytes 64516
  12.3 205.7 %all-to-all-start = ((bf16[32,256,256]{1,2,0:T(8,128)(2,1)}), bf16[32,256,256]{1,2,0:T(8,128)(2,1)}, u32[]{:S(2)}, u32[]{:S(2)}) async-start(bf16[32,256,256]{1,2,0:T(8,128)(2,1)} %stack.2), calls=%async_computation | async-start | bytes 8388608 | tf_op jit(solution)/shard_map/all_to_all | solution.py:25
  218.0 13.0 %copy-start.1 = (f32[7,256]{1,0:T(8,128)S(1)}, f32[7,256]{1,0:T(8,128)}, u32[]{:S(2)}) copy-start(f32[7,256]{1,0:T(8,128)} %param.7) | copy-start | bytes 21508
  227.5 9.7 %collective-permute-start = (bf16[6,3,256]{0,2,1:T(8,128)(2,1)S(1)}, bf16[6,3,256]{0,2,1:T(8,128)(2,1)S(1)}, u32[]{:S(2)}, u32[]{:S(2)}) collective-permute-start(bf16[6,3,256]{0,2,1:T(8,128)(2,1)S(1)} %bitcast.39), channel_id=1, source_target_pairs={{0,32},{32,64},{64,96},{96,128},{128,160},{160,192},{192,224},{224... | collective-permute-start | bytes 27656 | tf_op jit(solution)/shard_map/ppermute | solution.py:10
  240.1 9.0 %collective-permute-start.1 = (f32[6,256]{0,1:T(8,128)S(1)}, f32[6,256]{0,1:T(8,128)S(1)}, u32[]{:S(2)}, u32[]{:S(2)}) collective-permute-start(f32[6,256]{0,1:T(8,128)S(1)} %slice_bitcast_fusion.1), channel_id=1, source_target_pairs={{0,32},{32,64},{64,96},{96,128},{128,160},{160,192},{192,224},{224... | collective-permute-start | bytes 18440 | tf_op jit(solution)/shard_map/ppermute | solution.py:10
Sparse Core Ops, SparseCore 0:
  10.3 118.6 all-gather.1
